TPU v7x, 32 devices: a whole 2x2x4 slice. The times are simulated.
32 devices in a mesh: site: 2 (over y), pt: 4 (over z), var: 2 (over x), cmp: 2 (over core).
Axes of the slice: x: 2, y: 2, z: 4, core: 2. Of those that a mesh axis runs over, the one named last changes fastest.
Arguments:
- strain_green: bfloat16 [5120, 24, 256], P(('site', 'pt'), None, 'cmp'), parts along dimension 0, may hold values from -2.390625 to 2.390625
- green_scale: float32 [40, 24], P(('site', 'pt')), parts along dimension 0, may hold values from 0.3 to 3
- mechanism: float32 [6, 2560], P(None, 'pt'), may hold values from -4 to 4
- slip_amplitude: bfloat16 [4, 32, 1536], P('pt', 'var'), may hold values from 0.19921875 to 2
- onset_time: float32 [4, 32, 1536], P('pt', 'var'), may hold values from 0 to 128
- rupture_row: int32 [4], replicated, may hold values from 0 to 3, each once
- rupture_blocks: int32 [4, 12], replicated, may hold values from 0 to 19, as said below
- block_count: int32 [4], replicated, may hold values from 1 to 12, 16 in all
- crossover: int32 [4], replicated, may hold values from 128 to 251
- high_band: float32 [8, 32, 2, 512], P(('site', 'pt'), 'var', None, 'cmp'), parts along dimension 0, may hold values from -6 to 6
Outputs:
- seismograms: float32 [8, 32, 2, 512], P(('site', 'pt'), 'var', None, 'cmp'), parts along dimension 0
There are 2 independent parts, one for each index of `site`. A program takes and returns all parts, laid end to end along the dimension named above; an argument that names none is the same for every part. Nothing has to cross between parts.
Inputs may be any that keep to these rules, and one draw needn't show every extreme that they name: `rupture_blocks`: each row names 12 different point blocks; rupture r covers the first block_count[r] of them.
All inputs are finite; a program needn't handle non-finite values.
Results may differ from a plain program's by a relative error of at most 0.0028.
Values may be sent and summed in bfloat16 or wider, within the bound.
A program may use at most 64 MiB of HBM per device.

v0:
```python
import math

import jax
import jax.numpy as jnp
from jax import lax
from jax.sharding import PartitionSpec as P

taper_width = 8.0


def green_tensor(strain_green, green_scale, mechanism):
    points = strain_green.shape[0]
    bins_here = strain_green.shape[2]
    blocks_scale = jnp.repeat(green_scale, points // green_scale.shape[0], axis=0)
    factors = blocks_scale.reshape(points, 4, 6) * jnp.transpose(mechanism)[:, None, :]
    spectra = strain_green.reshape(points, 4, 6, bins_here).astype(jnp.float32)
    summed = jnp.einsum("pkjf,pkj->pkf", spectra, factors, precision=lax.Precision.HIGHEST)
    return summed.astype(jnp.bfloat16)


def block_term(green_block, amplitude, onset_block, phase_step):
    angles = onset_block[:, :, None] * phase_step[None, None, :]
    weight = amplitude.astype(jnp.float32)[:, :, None]
    with_cos = weight * jnp.cos(angles)
    with_sin = weight * jnp.sin(angles)
    real_list = []
    imag_list = []
    for component in range(2):
        real_green = green_block[:, component, :][None, :, :]
        imag_green = green_block[:, 2 + component, :][None, :, :]
        real_list.append(jnp.sum(with_cos * real_green + with_sin * imag_green, axis=1))
        imag_list.append(jnp.sum(with_cos * imag_green - with_sin * real_green, axis=1))
    return jnp.stack(real_list + imag_list, axis=1)


def live_pairs(blocks, covered, lowest, beyond):
    slot_total = blocks.shape[1]
    slot_ids = jnp.arange(slot_total)[None, :]
    inside = (slot_ids < covered[:, None]) & (blocks >= lowest) & (blocks < beyond)
    live_flags = inside.reshape(-1).astype(jnp.int32)
    ordering = jnp.argsort(1 - live_flags, stable=True)
    return (ordering, jnp.sum(live_flags))


def accumulate(
    running,
    ordering,
    number_live,
    slot_total,
    fetch_green,
    amplitudes,
    onsets,
    phase_step,
    block_points,
):

    def visit(counter, running):
        pair_number = ordering[counter]
        row_number = pair_number // slot_total
        slot_number = pair_number % slot_total
        green_block = fetch_green(row_number, slot_number)
        offset = slot_number * block_points
        amplitude = lax.dynamic_slice_in_dim(amplitudes[row_number], offset, block_points, 1)
        onset_block = lax.dynamic_slice_in_dim(onsets[row_number], offset, block_points, 1)
        contribution = block_term(green_block, amplitude, onset_block, phase_step)
        current = lax.dynamic_index_in_dim(running, row_number, 0, keepdims=False)
        return lax.dynamic_update_index_in_dim(running, current + contribution, row_number, 0)

    return lax.fori_loop(0, number_live, visit, running)


def body(
    strain_green,
    green_scale,
    mechanism,
    slip_amplitude,
    onset_time,
    rupture_row,
    rupture_blocks,
    block_count,
    crossover,
    high_band,
):
    highest = lax.Precision.HIGHEST
    points_here = strain_green.shape[0]
    bins_here = strain_green.shape[2]
    blocks_here = green_scale.shape[0]
    block_points = points_here // blocks_here
    rows_here = slip_amplitude.shape[0]
    variations = slip_amplitude.shape[1]
    slot_total = slip_amplitude.shape[2] // block_points
    bin_half = lax.axis_index("cmp")
    samples = 2 * bins_here * lax.axis_size("cmp")
    bins_global = bin_half * bins_here + jnp.arange(bins_here)
    frequency = bins_global.astype(jnp.float32)
    phase_step = frequency * (2.0 * math.pi / samples)
    green_blocks = green_tensor(strain_green, green_scale, mechanism).reshape(
        blocks_here, block_points, 4, bins_here
    )
    first_row = lax.axis_index("pt") * rows_here
    own_ruptures = lax.dynamic_slice_in_dim(rupture_row, first_row, rows_here, 0)
    all_amplitudes, all_onsets = (
        lax.all_gather(slip_amplitude.astype(jnp.float32), "pt", axis=0, tiled=True).astype(
            slip_amplitude.dtype
        ),
        lax.all_gather(onset_time, "pt", axis=0, tiled=True),
    )
    lowest = lax.axis_index("pt") * blocks_here
    blocks = rupture_blocks[rupture_row]
    ordering, number_live = live_pairs(
        blocks, block_count[rupture_row], lowest, lowest + blocks_here
    )

    def fetch_green(row_number, slot_number):
        return lax.dynamic_index_in_dim(
            green_blocks, blocks[row_number, slot_number] - lowest, 0, keepdims=False
        )

    initial = jnp.zeros((rows_here * lax.axis_size("pt"), variations, 4, bins_here), jnp.float32)
    spectrum = lax.psum_scatter(
        accumulate(
            initial,
            ordering,
            number_live,
            slot_total,
            fetch_green,
            all_amplitudes,
            all_onsets,
            phase_step,
            block_points,
        ),
        "pt",
        scatter_dimension=0,
        tiled=True,
    )
    all_band = lax.all_gather(high_band, "cmp", axis=3, tiled=True)
    sample_ids = jnp.arange(samples)
    angles = (bins_global[:, None] * sample_ids[None, :] % samples).astype(jnp.float32) * (
        2.0 * math.pi / samples
    )
    cosine = jnp.cos(angles)
    sine_table = jnp.sin(angles)
    band_rows = all_band.reshape(-1, samples)
    band_real = jnp.dot(band_rows, cosine.T, precision=highest)
    band_imag = -jnp.dot(band_rows, sine_table.T, precision=highest)
    crossing = crossover[own_ruptures].astype(jnp.float32)
    taper_weight = jnp.clip((crossing[:, None] - frequency[None, :]) / taper_width + 0.5, 0.0, 1.0)
    taper_rows = jnp.repeat(taper_weight, variations * 2, axis=0)
    spectrum_real = spectrum[:, :, 0:2].reshape(-1, bins_here)
    spectrum_imag = spectrum[:, :, 2:4].reshape(-1, bins_here)
    coefficient = jnp.where(bins_global == 0, 1.0, 2.0) / samples
    excess_real = taper_rows * (spectrum_real - band_real) * coefficient
    excess_imag = taper_rows * (spectrum_imag - band_imag) * coefficient
    basis_table = jnp.concatenate([cosine, -sine_table], axis=0)
    partial_value = jnp.dot(
        jnp.concatenate([excess_real, excess_imag], axis=1), basis_table, precision=highest
    )
    partial_value = partial_value.reshape(rows_here, variations, 2, samples)
    low_band = lax.psum_scatter(partial_value, "cmp", scatter_dimension=3, tiled=True)
    return high_band + low_band


def solution(mesh):
    return jax.shard_map(
        body,
        mesh=mesh,
        in_specs=(
            P(("site", "pt"), None, "cmp"),
            P(("site", "pt"), None),
            P(None, "pt"),
            P("pt", "var", None),
            P("pt", "var", None),
            P(),
            P(),
            P(),
            P(),
            P(("site", "pt"), "var", None, "cmp"),
        ),
        out_specs=P(("site", "pt"), "var", None, "cmp"),
        check_vma=False,
    )
```

profile of v0, /device:TPU:0, one launch (start us, length us, event | category | flops | bytes accessed | tf_op | source)
XLA Modules:
  0.0 168.7 jit_solution(17201936582558625197)
XLA Ops:
  6.5 0.7 compare_select_fusion
  7.8 1.3 gather_fusion
  9.9 4.9 %copy.24 = bf16[640,24,128]{2,0,1:T(8,128)(2,1)} copy(bf16[640,24,128]{2,1,0:T(8,128)(2,1)} %param.12) | data formatting | bytes 7864320 | tf_op args[0]
  15.0 1.3 copy.28
  16.4 16.4 %fusion.25 = bf16[640,4,1,128]{3,2,1,0:T(2,128)(2,1)S(1)} fusion(f32[640,4,6,1]{2,3,1,0:T(1,128)S(1)} %copy.28, bf16[640,4,6,128]{3,0,2,1:T(8,128)(2,1)} %bitcast.100), kind=kOutput, calls=%fused_computation.37 | convolution fusion | flops 23592960 | bytes 4648960 | tf_op jit(solution)/shard_map/pkjf,pkj->pkf/dot_general | solution.py:17
  33.0 16.3 %all_gather.10 = f32[4,16,1536]{2,1,0:T(8,128)S(1)} all-gather(f32[1,16,1536]{2,1,0:T(8,128)S(1)} %copy-done.3), channel_id=1, replica_groups=mesh['site'=2,'pt'=4,'var'=2,'cmp'=2] {'pt'}, dimensions={0}, use_global_device_ids=true | all-gather | bytes 491520 | tf_op jit(solution)/shard_map/all_gather | solution.py:106
  49.2 14.2 %all_gather.9 = bf16[4,16,1536]{2,1,0:T(8,128)(2,1)S(1)} all-gather(bf16[1,16,1536]{2,1,0:T(8,128)(2,1)S(1)} %copy-done.4), channel_id=1, replica_groups=mesh['site'=2,'pt'=4,'var'=2,'cmp'=2] {'pt'}, dimensions={0}, use_global_device_ids=true | all-gather | bytes 245760 | tf_op jit(solution)/shard_map/all_gather | solution.py:103
  63.5 2.1 %sort.17 = (s32[48]{0:T(128)}, s32[48]{0:T(128)S(1)}) sort(s32[48]{0:T(128)S(1)} %reshape.190, s32[48]{0:T(128)S(1)} %iota.20), dimensions={0}, to_apply=%region_1.2 | sort | flops 288 | bytes 768 | tf_op jit(solution)/shard_map/jit(argsort)/sort | solution.py:41
  65.6 42.6 %while.15 = (s32[]{:T(128)}, f32[4,16,4,128]{3,1,2,0:T(8,128)S(1)}, s32[]{:T(128)}, s32[48]{0:T(128)S(1)}, bf16[4,16,1536]{2,1,0:T(8,128)(2,1)S(1)}, /*index=5*/...) while((s32[]{:T(128)}, f32[4,16,4,128]{3,1,2,0:T(8,128)S(1)}, ...), condition=%wide.region_7.8_spmd.clone, body=%wide.region_2.7_spmd.clone.sunk | while | flops 5073313 | bytes 1095254 | solution.py:69
  70.7 5.5 %fusion.73 = (f32[16,128]{1,0:T(8,128)S(1)}, f32[16,128]{1,0:T(8,128)S(1)}, f32[16,128]{1,0:T(8,128)S(1)}, f32[16,128]{1,0:T(8,128)S(1)}) fusion(f32[128,128]{1,0:T(8,128)S(1)} %get-tuple-element.330, f32[128,128]{1,0:T(8,128)S(1)} %get-tuple-element.331, f32[128]{0:T(128)S(1)} %convert_multiply_fusion.2, ...), kind=kLoop, calls=%fused_computation.11.clone.1 | loop fusion | flops 4972544 | bytes 311808 | tf_op jit(solution)/shard_map/while/body/reduce_sum | solution.py:31
  81.2 5.5 %fusion.73 = (f32[16,128]{1,0:T(8,128)S(1)}, f32[16,128]{1,0:T(8,128)S(1)}, f32[16,128]{1,0:T(8,128)S(1)}, f32[16,128]{1,0:T(8,128)S(1)}) fusion(f32[128,128]{1,0:T(8,128)S(1)} %get-tuple-element.330, f32[128,128]{1,0:T(8,128)S(1)} %get-tuple-element.331, f32[128]{0:T(128)S(1)} %convert_multiply_fusion.2, ...), kind=kLoop, calls=%fused_computation.11.clone.1 | loop fusion | flops 4972544 | bytes 311808 | tf_op jit(solution)/shard_map/while/body/reduce_sum | solution.py:31
  91.7 5.5 %fusion.73 = (f32[16,128]{1,0:T(8,128)S(1)}, f32[16,128]{1,0:T(8,128)S(1)}, f32[16,128]{1,0:T(8,128)S(1)}, f32[16,128]{1,0:T(8,128)S(1)}) fusion(f32[128,128]{1,0:T(8,128)S(1)} %get-tuple-element.330, f32[128,128]{1,0:T(8,128)S(1)} %get-tuple-element.331, f32[128]{0:T(128)S(1)} %convert_multiply_fusion.2, ...), kind=kLoop, calls=%fused_computation.11.clone.1 | loop fusion | flops 4972544 | bytes 311808 | tf_op jit(solution)/shard_map/while/body/reduce_sum | solution.py:31
  102.2 5.5 %fusion.73 = (f32[16,128]{1,0:T(8,128)S(1)}, f32[16,128]{1,0:T(8,128)S(1)}, f32[16,128]{1,0:T(8,128)S(1)}, f32[16,128]{1,0:T(8,128)S(1)}) fusion(f32[128,128]{1,0:T(8,128)S(1)} %get-tuple-element.330, f32[128,128]{1,0:T(8,128)S(1)} %get-tuple-element.331, f32[128]{0:T(128)S(1)} %convert_multiply_fusion.2, ...), kind=kLoop, calls=%fused_computation.11.clone.1 | loop fusion | flops 4972544 | bytes 311808 | tf_op jit(solution)/shard_map/while/body/reduce_sum | solution.py:31
  112.8 2.1 %all_gather.11 = f32[1,16,2,512]{3,2,1,0:T(2,128)S(1)} all-gather(f32[1,16,2,256]{3,2,1,0:T(2,128)S(1)} %copy-done.2), channel_id=1, replica_groups=mesh['site'=2,'pt'=4,'var'=2,'cmp'=2] {'cmp'}, dimensions={3}, use_global_device_ids=true | all-gather | bytes 98304 | tf_op jit(solution)/shard_map/all_gather | solution.py:136
  114.9 1.1 fusion.45
  116.0 24.1 %reduce-scatter.5.cloned.1.call-done = f32[1,16,4,128]{3,1,2,0:T(8,128)} async-done(((f32[4,16,4,128]{3,1,2,0:T(8,128)}), f32[1,16,4,128]{3,1,2,0:T(8,128)}) %reduce-scatter.5.cloned.1.call-update) | async-done | bytes 32784 | tf_op jit(solution)/shard_map/reduce_scatter | solution.py:120
  140.1 0.7 fusion.65
  140.9 1.4 fusion.32
  142.3 1.4 fusion.33
  144.1 3.4 %copy.31 = f32[1,16,2,512]{2,1,0,3:T(8,128)} copy(f32[1,16,2,512]{3,2,1,0:T(2,128)S(1)} %reshape.161) | data formatting | bytes 131072
  147.6 4.3 %reshape.216 = f32[512,32]{1,0:T(8,128)} reshape(f32[512,1,16,2]{3,2,1,0:T(8,128)} %bitcast.98) | data formatting | bytes 131072
  151.8 6.1 %reduce-scatter.7.cloned.1.call-done = f32[256,32]{1,0:T(8,128)} async-done(((f32[512,32]{1,0:T(8,128)}), f32[256,32]{1,0:T(8,128)}) %reduce-scatter.7.cloned.1.call-update) | async-done | bytes 32784
  157.9 2.1 %reshape.217 = f32[256,1,16,2]{3,2,1,0:T(8,128)S(1)} reshape(f32[256,32]{1,0:T(8,128)} %reduce-scatter.7.cloned.1.call-done) | data formatting | bytes 65536
  160.1 1.1 copy.32
  (76 shorter events, 11.1 us)
Async XLA Ops:
  6.5 0.7 copy-start
  6.5 133.6 %reduce-scatter.5.cloned.1.call-start = ((), (), s32[]{:S(2)}) async-start(), calls=%async_computation.2 | async-start | bytes 163840 | tf_op jit(solution)/shard_map/reduce_scatter | solution.py:120
  9.9 4.9 %copy-start.6 = (f32[5,24]{1,0:T(8,128)S(1)}, f32[5,24]{1,0:T(8,128)}, u32[]{:S(2)}) copy-start(f32[5,24]{1,0:T(8,128)} %param.13) | copy-start | bytes 1444
  9.9 5.1 %copy-start.5 = (f32[6,640]{1,0:T(8,128)S(1)}, f32[6,640]{1,0:T(8,128)}, u32[]{:S(2)}) copy-start(f32[6,640]{1,0:T(8,128)} %param.14) | copy-start | bytes 46084
  16.4 16.6 %copy-start.3 = (f32[1,16,1536]{2,1,0:T(8,128)S(1)}, f32[1,16,1536]{2,1,0:T(8,128)}, u32[]{:S(2)}) copy-start(f32[1,16,1536]{2,1,0:T(8,128)} %param.16) | copy-start | bytes 294916
  16.4 32.9 %copy-start.4 = (bf16[1,16,1536]{2,1,0:T(8,128)(2,1)S(1)}, bf16[1,16,1536]{2,1,0:T(8,128)(2,1)}, u32[]{:S(2)}) copy-start(bf16[1,16,1536]{2,1,0:T(8,128)(2,1)} %param.15) | copy-start | bytes 147460
  65.6 43.4 %copy-start.7 = (s32[4]{0:T(128)S(1)}, s32[4]{0:T(128)}, u32[]{:S(2)}) copy-start(s32[4]{0:T(128)} %param.17) | copy-start | bytes 52
  65.6 45.9 %copy-start.8 = (s32[4]{0:T(128)S(1)}, s32[4]{0:T(128)}, u32[]{:S(2)}) copy-start(s32[4]{0:T(128)} %param.20) | copy-start | bytes 52
  65.6 47.2 %copy-start.2 = (f32[1,16,2,256]{3,2,1,0:T(2,128)S(1)}, f32[1,16,2,256]{3,2,1,0:T(2,128)}, u32[]{:S(2)}) copy-start(f32[1,16,2,256]{3,2,1,0:T(2,128)} %param.21) | copy-start | bytes 98308
  108.3 0.6 copy-start.1
  108.9 49.0 %reduce-scatter.7.cloned.1.call-start = ((), (), s32[]{:S(2)}) async-start(), calls=%async_computation.3 | async-start | bytes 393216
Sparse Core Ops, SparseCore 0:
  109.0 31.0 reduce-scatter.4
  152.0 5.9 reduce-scatter.6
where the time goes:
time: 169 us
  blocking collectives  32.6 us (19%)
  waiting for transfers between devices  30.2 us (18%)
  local copies, waits for them, and re-layouts  27.9 us (17%)
  other arithmetic  27.6 us (16%)
  matrix products  19.6 us (12%)
  between operations  16.2 us (10%)
  loops' own time  14.6 us (9%)
    reduce_scatter x1, waiting for transfers between devices, body(): lax.psum_scatter(accumulate(initial, ordering, number_live, slot_total, f...  24.1 us
    reduce_sum x4, other arithmetic, block_term(): jnp.sum(with_cos * real_green + with_sin * imag_green, axis=1)  21.8 us
    unnamed x24, local copies, waits for them, and re-layouts  16.6 us
    dot_general x1, matrix products, green_tensor(): jnp.einsum('pkjf,pkj->pkf', spectra, factors, precision=lax.Precision.HIG...  16.4 us
    all_gather x1, blocking collectives, body(): lax.all_gather(onset_time, 'pt', axis=0, tiled=True)  16.3 us
    another operation x1, loops' own time, accumulate(): return lax.fori_loop(0, number_live, visit, running)  14.6 us
    all_gather x1, blocking collectives, body(): lax.all_gather(slip_amplitude.astype(jnp.float32), 'pt', axis=0, tiled=True)  14.2 us
    unnamed x3, waiting for transfers between devices  6.11 us
  transfers between devices with their start and end apart: 2, of which 2 were waited for; matrix products, arithmetic and copies ran while one was open for 1% of the time, Pallas kernels for 0%

commit v1 on v0

v1 whole, which is shorter than its diff:
```python
import functools
import math

import jax
import jax.numpy as jnp
import numpy as np
from jax import lax
from jax.experimental import pallas as pl
from jax.experimental.pallas import tpu as pltpu
from jax.sharding import PartitionSpec as P

taper_width = 8.0
MESH = pl.DeviceIdType.MESH
VMEM = pltpu.VMEM
SMEM = pltpu.SMEM


def column_bins(bins_here):
    half = bins_here // 2
    column = np.arange(2 * bins_here)
    return (column // bins_here) * half + column % half, (column // half) % 2


def basis_tables(bins_here, parts, samples):
    bins, imaginary = column_bins(bins_here)
    time = np.arange(samples)[:, None]
    tables = []
    for part in range(parts):
        angle = ((part * bins_here + bins)[None, :] * time % samples) * (2.0 * math.pi / samples)
        tables.append(np.where(imaginary[None, :] == 1, -np.sin(angle), np.cos(angle)))
    exact = np.stack(tables)
    upper = exact.astype(jnp.bfloat16)
    lower = (exact - upper.astype(np.float64)).astype(jnp.bfloat16)
    return np.stack([upper, lower], axis=1)


def wide_dot(rows, upper, lower, dims):
    head = rows.astype(jnp.bfloat16)
    tail = (rows - head.astype(jnp.float32)).astype(jnp.bfloat16)
    dot = functools.partial(
        lax.dot_general, dimension_numbers=(dims, ((), ())), preferred_element_type=jnp.float32
    )
    return dot(head, upper) + (dot(head, lower) + dot(tail, upper))


def greet(peers):
    barrier = pltpu.get_barrier_semaphore()
    for peer in peers:
        pl.semaphore_signal(barrier, inc=1, device_id=peer, device_id_type=MESH)
    pl.semaphore_wait(barrier, len(peers))


def others(me, count):
    return [{"pt": lax.rem(me + step, count)} for step in range(1, count)]


def gather_kernel(
    count,
    strain_ref,
    scale_ref,
    mechanism_ref,
    slip_ref,
    onset_ref,
    band_ref,
    table_hbm,
    weights_ref,
    slips_ref,
    onsets_ref,
    spectrum_ref,
    strain_buf,
    wide_buf,
    table_buf,
    band_send,
    band_peer,
    local_sem,
    strain_sem,
    send_sem,
    recv_sem,
):
    me = lax.axis_index("pt")
    part = lax.axis_index("cmp")
    partner = {"cmp": 1 - part}
    blocks_here = scale_ref.shape[0]
    block = strain_ref.shape[0] // blocks_here
    bins = strain_ref.shape[2]
    half = bins // 2
    own = band_ref.shape[3]
    variations = band_ref.shape[1]
    strain_copies = []
    for b in range(blocks_here):
        rows = pl.ds(b * block, block)
        copy = pltpu.make_async_copy(strain_ref.at[rows], strain_buf.at[rows], strain_sem.at[b])
        copy.start()
        strain_copies.append(copy)
    table_copy = pltpu.make_async_copy(table_hbm.at[part], table_buf, local_sem.at[2])
    table_copy.start()
    keep = [
        pltpu.make_async_copy(slip_ref, slips_ref.at[pl.ds(me, 1)], local_sem.at[0]),
        pltpu.make_async_copy(onset_ref, onsets_ref.at[pl.ds(me, 1)], local_sem.at[1]),
    ]
    for copy in keep:
        copy.start()
    for c in range(2):
        band_send[pl.ds(c * variations, variations), :] = band_ref[0, :, c, :]
    greet(others(me, count) + [partner])
    sends = []
    for step, peer in enumerate(others(me, count)):
        for which, (source, target) in enumerate(((onset_ref, onsets_ref), (slip_ref, slips_ref))):
            copy = pltpu.make_async_remote_copy(
                src_ref=source,
                dst_ref=target.at[pl.ds(me, 1)],
                send_sem=send_sem.at[2 * step + which],
                recv_sem=recv_sem.at[2 * step + which],
                device_id=peer,
                device_id_type=MESH,
            )
            copy.start()
            sends.append(copy)
    band_copy = pltpu.make_async_remote_copy(
        src_ref=band_send,
        dst_ref=band_peer,
        send_sem=send_sem.at[2 * (count - 1)],
        recv_sem=recv_sem.at[2 * (count - 1)],
        device_id=partner,
        device_id_type=MESH,
    )
    band_copy.start()

    low_lanes = lax.broadcasted_iota(jnp.int32, (block, bins), 1) < half
    for b in range(blocks_here):
        strain_copies[b].wait()
        wide_buf[...] = (
            strain_buf[pl.ds(b * block, block)].astype(jnp.float32).reshape(block * 24, bins)
        )
        moment = mechanism_ref[:, pl.ds(b * block, block)]
        factors = jnp.transpose(jnp.concatenate([moment] * 4, axis=0)) * scale_ref[pl.ds(b, 1), :]
        for c in range(2):
            green = []
            for ri in range(2):
                total = None
                for j in range(6):
                    row = 12 * ri + 6 * c + j
                    term = factors[:, row : row + 1] * wide_buf[pl.ds(row, block, stride=24), :]
                    total = term if total is None else total + term
                green.append(total)
            real, imag = green
            real_turned = pltpu.roll(real, half, 1)
            imag_turned = pltpu.roll(imag, half, 1)
            lanes = pl.ds(c * bins, bins)
            pieces = (
                (0, 0, real, imag_turned),
                (0, 1, imag, -real_turned),
                (1, 0, real_turned, imag),
                (1, 1, imag_turned, -real),
            )
            for which, lower, first, second in pieces:
                weights_ref[b, which, pl.ds(lower * block, block), lanes] = jnp.where(
                    low_lanes, first, second
                ).astype(jnp.bfloat16)

    table_copy.wait()
    band_copy.wait()
    mine = pl.ds(pl.multiple_of(part * own, own), own)
    theirs = pl.ds(pl.multiple_of((1 - part) * own, own), own)
    down = ((1,), (0,))
    spectrum_ref[...] = wide_dot(
        band_send[...], table_buf[0, mine, :], table_buf[1, mine, :], down
    ) + wide_dot(band_peer[...], table_buf[0, theirs, :], table_buf[1, theirs, :], down)
    for copy in keep:
        copy.wait()
    for copy in sends:
        copy.wait()


def turn(first, second):
    return (
        first[0] * second[0] - first[1] * second[1],
        first[0] * second[1] + first[1] * second[0],
    )


def pair_kernel(
    step_angle,
    row_ref,
    blocks_ref,
    covered_ref,
    weights_ref,
    slips_ref,
    onsets_ref,
    partial_ref,
    total_ref,
):
    me = lax.axis_index("pt")
    part = lax.axis_index("cmp")
    blocks_here, halves, depth, columns = weights_ref.shape
    rows, variations, unused = slips_ref.shape
    block = depth // 2
    bins = columns // 2
    half = bins // 2
    fine_total = 16
    lowest = me * blocks_here
    lane_bin = lax.broadcasted_iota(jnp.int32, (variations, columns), 1) % half

    def one_row(row, carry):
        rupture = row_ref[row]
        total_ref[...] = jnp.zeros_like(total_ref)

        def one_slot(slot, carry):
            local = blocks_ref[rupture, slot] - lowest

            @pl.when((local >= 0) & (local < blocks_here))
            def _():
                lanes = pl.ds(pl.multiple_of(slot * block, block), block)
                angle = onsets_ref[row, :, lanes] * step_angle
                amplitude = slips_ref[row, :, lanes].astype(jnp.float32)
                powers = [None, (jnp.cos(angle), jnp.sin(angle))]
                for k in range(2, fine_total + 1):
                    powers.append(turn(powers[k // 2], powers[k - k // 2]))
                leap = powers[fine_total]
                far = leap
                for unused in range(int(math.log2(bins // fine_total))):
                    far = turn(far, far)
                second_part = part == 1
                coarse = (
                    amplitude * jnp.where(second_part, far[0], 1.0),
                    amplitude * jnp.where(second_part, far[1], 0.0),
                )
                per_half = half // fine_total
                for which in range(halves):
                    found = jnp.zeros((variations, columns), jnp.float32)
                    for h in range(per_half):
                        pieces = []
                        for k in range(fine_total):
                            phase = coarse if k == 0 else turn(coarse, powers[k])
                            pieces.append(
                                jnp.concatenate(
                                    [phase[0].astype(jnp.bfloat16), phase[1].astype(jnp.bfloat16)],
                                    axis=1,
                                )
                            )
                        product = jnp.dot(
                            jnp.concatenate(pieces, axis=0),
                            weights_ref[local, which],
                            preferred_element_type=jnp.float32,
                        )
                        for k in range(fine_total):
                            found = jnp.where(
                                lane_bin == h * fine_total + k,
                                product[k * variations : (k + 1) * variations],
                                found,
                            )
                        coarse = turn(coarse, leap)
                    total_ref[which] += found

            return carry

        lax.fori_loop(0, covered_ref[rupture], one_slot, 0)
        partial_ref[row] = total_ref[...].astype(jnp.bfloat16)
        return carry

    lax.fori_loop(0, rows, one_row, 0)


def merge_kernel(
    count,
    row_ref,
    crossover_ref,
    partial_ref,
    spectrum_ref,
    band_ref,
    table_hbm,
    out_ref,
    arrived,
    table_buf,
    low_send,
    low_peer,
    local_sem,
    send_sem,
    recv_sem,
):
    me = lax.axis_index("pt")
    part = lax.axis_index("cmp")
    partner = {"cmp": 1 - part}
    own = band_ref.shape[3]
    bins = partial_ref.shape[3] // 2
    half = bins // 2
    variations = partial_ref.shape[2]
    table_copy = pltpu.make_async_copy(table_hbm.at[part], table_buf, local_sem)
    table_copy.start()
    greet(others(me, count) + [partner])
    sends = []
    for step, peer in enumerate(others(me, count)):
        copy = pltpu.make_async_remote_copy(
            src_ref=partial_ref.at[peer["pt"]],
            dst_ref=arrived.at[step],
            send_sem=send_sem.at[step],
            recv_sem=recv_sem.at[step],
            device_id=peer,
            device_id_type=MESH,
        )
        copy.start()
        sends.append(copy)
    crossing = crossover_ref[row_ref[me]].astype(jnp.float32)
    column = lax.broadcasted_iota(jnp.int32, (variations, 2 * bins), 1)
    frequency_id = part * bins + (column // bins) * half + column % half
    frequency = frequency_id.astype(jnp.float32)
    taper = jnp.clip((crossing - frequency) / taper_width + 0.5, 0.0, 1.0)
    weight = taper * jnp.where(frequency_id == 0, 1.0, 2.0) / table_buf.shape[1]
    table_copy.wait()
    total = partial_ref[me].astype(jnp.float32)
    for step, copy in enumerate(sends):
        copy.wait()
        total = total + arrived[step].astype(jnp.float32)
    excess = []
    for c in range(2):
        lanes = slice(c * bins, (c + 1) * bins)
        spectrum = jnp.concatenate([total[0][:, lanes], total[1][:, lanes]], axis=1)
        here = pl.ds(c * variations, variations)
        excess.append((spectrum - spectrum_ref[here, :]) * weight)
    rows = jnp.concatenate(excess, axis=0)
    mine = pl.ds(pl.multiple_of(part * own, own), own)
    theirs = pl.ds(pl.multiple_of((1 - part) * own, own), own)
    across = ((1,), (1,))
    low_send[...] = wide_dot(rows, table_buf[0, theirs, :], table_buf[1, theirs, :], across)
    exchange = pltpu.make_async_remote_copy(
        src_ref=low_send,
        dst_ref=low_peer,
        send_sem=send_sem.at[count - 1],
        recv_sem=recv_sem.at[count - 1],
        device_id=partner,
        device_id_type=MESH,
    )
    exchange.start()
    low = wide_dot(rows, table_buf[0, mine, :], table_buf[1, mine, :], across)
    exchange.wait()
    low = low + low_peer[...]
    for c in range(2):
        out_ref[0, :, c, :] = band_ref[0, :, c, :] + low[c * variations : (c + 1) * variations]


def body(
    strain_green,
    green_scale,
    mechanism,
    slip_amplitude,
    onset_time,
    rupture_row,
    rupture_blocks,
    block_count,
    crossover,
    high_band,
):
    points, unused, bins = strain_green.shape
    blocks_here = green_scale.shape[0]
    block = points // blocks_here
    rows_here, variations, slots = slip_amplitude.shape
    count = lax.axis_size("pt")
    parts = lax.axis_size("cmp")
    own = high_band.shape[3]
    samples = own * parts
    rows = rows_here * count
    tables = jnp.asarray(basis_tables(bins, parts, samples))
    vmem = pl.BlockSpec(memory_space=VMEM)
    smem = pl.BlockSpec(memory_space=SMEM)
    anywhere = pl.BlockSpec(memory_space=pl.ANY)
    copies = 2 * (count - 1) + 1
    weights, slips, onsets, band_spectrum = pl.pallas_call(
        functools.partial(gather_kernel, count),
        out_shape=(
            jax.ShapeDtypeStruct((blocks_here, 2, 2 * block, 2 * bins), jnp.bfloat16),
            jax.ShapeDtypeStruct((rows, variations, slots), slip_amplitude.dtype),
            jax.ShapeDtypeStruct((rows, variations, slots), onset_time.dtype),
            jax.ShapeDtypeStruct((2 * variations, 2 * bins), jnp.float32),
        ),
        in_specs=[anywhere, vmem, vmem, vmem, vmem, vmem, anywhere],
        out_specs=(vmem, anywhere, anywhere, vmem),
        scratch_shapes=[
            VMEM(strain_green.shape, strain_green.dtype),
            VMEM((block * 24, bins), jnp.float32),
            VMEM((2, samples, 2 * bins), jnp.bfloat16),
            VMEM((2 * variations, own), jnp.float32),
            VMEM((2 * variations, own), jnp.float32),
            pltpu.SemaphoreType.DMA((3,)),
            pltpu.SemaphoreType.DMA((blocks_here,)),
            pltpu.SemaphoreType.DMA((copies,)),
            pltpu.SemaphoreType.DMA((copies,)),
        ],
        compiler_params=pltpu.CompilerParams(collective_id=0, has_side_effects=True),
        name="gather",
    )(strain_green, green_scale, mechanism, slip_amplitude, onset_time, high_band, tables)
    partial_spectra = pl.pallas_call(
        functools.partial(pair_kernel, 2.0 * math.pi / samples),
        out_shape=jax.ShapeDtypeStruct((rows, 2, variations, 2 * bins), jnp.bfloat16),
        in_specs=[smem, smem, smem, vmem, vmem, vmem],
        out_specs=vmem,
        scratch_shapes=[VMEM((2, variations, 2 * bins), jnp.float32)],
        name="pairs",
    )(rupture_row, rupture_blocks, block_count, weights, slips, onsets)
    return pl.pallas_call(
        functools.partial(merge_kernel, count),
        out_shape=jax.ShapeDtypeStruct(high_band.shape, high_band.dtype),
        in_specs=[smem, smem, vmem, vmem, vmem, anywhere],
        out_specs=vmem,
        scratch_shapes=[
            VMEM((count - 1, 2, variations, 2 * bins), jnp.bfloat16),
            VMEM((2, samples, 2 * bins), jnp.bfloat16),
            VMEM((2 * variations, own), jnp.float32),
            VMEM((2 * variations, own), jnp.float32),
            pltpu.SemaphoreType.DMA(()),
            pltpu.SemaphoreType.DMA((count,)),
            pltpu.SemaphoreType.DMA((count,)),
        ],
        compiler_params=pltpu.CompilerParams(collective_id=1, has_side_effects=True),
        name="merge",
    )(rupture_row, crossover, partial_spectra, band_spectrum, high_band, tables)


def solution(mesh):
    return jax.shard_map(
        body,
        mesh=mesh,
        in_specs=(
            P(("site", "pt"), None, "cmp"),
            P(("site", "pt"), None),
            P(None, "pt"),
            P("pt", "var", None),
            P("pt", "var", None),
            P(),
            P(),
            P(),
            P(),
            P(("site", "pt"), "var", None, "cmp"),
        ),
        out_specs=P(("site", "pt"), "var", None, "cmp"),
        check_vma=False,
    )
```

time: 169 us -> 36 us (0.21)
  Pallas kernels: 0 us -> 34.4 us
  blocking collectives: 32.6 us -> 0 us
  waiting for transfers between devices: 30.2 us -> 0 us
  other arithmetic: 27.6 us -> 0 us
  local copies, waits for them, and re-layouts: 27.9 us -> 1.38 us
  matrix products: 19.6 us -> 0 us
  between operations: 16.2 us -> 0.02 us
  loops' own time: 14.6 us -> 0 us
    pallas_call x0 -> x3, Pallas kernels: none -> 34.4 us  [the longest x1 18.4 us: body(): pl.pallas_call(functools.partial(gather_kernel, count), out_shape=(jax.Sh...]
    all_gather x3 -> x0, blocking collectives: 32.6 us -> none  [the longest x1 16.3 us: body(): lax.all_gather(onset_time, 'pt', axis=0, tiled=True)]
    reduce_scatter x1 -> x0, waiting for transfers between devices: 24.1 us -> none  [body(): lax.psum_scatter(accumulate(initial, ordering, number_live, slot_total, f...]
    reduce_sum x5 -> x0, other arithmetic: 22.5 us -> none  [the longest x4 21.8 us: block_term(): jnp.sum(with_cos * real_green + with_sin * imag_green, axis=1)]
    dot_general x4 -> x0, matrix products: 19.6 us -> none  [the longest x1 16.4 us: green_tensor(): jnp.einsum('pkjf,pkj->pkf', spectra, factors, precision=lax.Precision.HIG...]
    unnamed x24 -> x1, local copies, waits for them, and re-layouts: 16.6 us -> 1.38 us
    another operation x1 -> x0, loops' own time: 14.6 us -> none  [accumulate(): return lax.fori_loop(0, number_live, visit, running)]
    unnamed x3 -> x0, waiting for transfers between devices: 6.11 us -> none
  transfers between devices with their start and end apart: 2 -> 0, of which waited for: 2 -> 0; matrix products, arithmetic and copies ran while one was open for 1% -> 0% of each run, Pallas kernels for 0% -> 0%
where the time goes in v1:
time: 36 us; the launch traced here: 35.8 us
  Pallas kernels  34.4 us (96%)
  local copies, waits for them, and re-layouts  1.38 us (4%)
    pallas_call x1, Pallas kernels, body(): pl.pallas_call(functools.partial(gather_kernel, count), out_shape=(jax.Sh...  18.4 us
    pallas_call x1, Pallas kernels, body(): pl.pallas_call(functools.partial(merge_kernel, count), out_shape=jax.Shap...  12.4 us
    pallas_call x1, Pallas kernels, body(): pl.pallas_call(functools.partial(pair_kernel, 2.0 * math.pi / samples), o...  3.55 us
    unnamed x1, local copies, waits for them, and re-layouts  1.38 us

profile of v1, /device:TPU:0, one launch (start us, length us, event | category | flops | bytes accessed | tf_op | source)
XLA Modules:
  0.0 35.8 jit_solution(12951220544464440850)
XLA Ops:
  0.0 18.4 %gather.1 = (bf16[5,2,256,256]{3,2,1,0:T(8,128)(2,1)}, bf16[4,16,1536]{2,1,0:T(8,128)(2,1)}, f32[4,16,1536]{2,1,0:T(8,128)}, f32[32,256]{1,0:T(8,128)}) custom-call(bf16[640,24,128]{2,1,0:T(8,128)(2,1)} %strain_ref.1, f32[5,24]{1,0:T(8,128)} %scale_ref.1, f32[6,640]{1,0:T(8,128)} %mechanism_ref.1, bf16[1,16,1536]{2,1,0:T(8,128)(2,1)} %slip_ref.1, ...), custom_call_target="tpu_custom_call" | custom-call | tf_op jit(solution)/shard_map/gather/pallas_call | solution.py:367
  18.4 3.5 %pairs.1.partial_ref = bf16[4,2,16,256]{3,2,1,0:T(8,128)(2,1)} custom-call(s32[4]{0:T(128)} %row_ref.3, s32[4,12]{1,0:T(4,128)} %blocks_ref.1, s32[4]{0:T(128)} %covered_ref.1, bf16[5,2,256,256]{3,2,1,0:T(8,128)(2,1)} %get-tuple-element.9.weights_ref, bf16[4,16,1536]{2,1,0:T(8,128)(2,1)} %get-tuple-element.10.slips_ref, ...), custom_call_target="tpu_custom_call" | custom-call | tf_op jit(solution)/shard_map/pairs/pallas_call | solution.py:391
  22.0 12.4 %merge.1 = f32[1,16,2,256]{3,2,1,0:T(2,128)} custom-call(s32[4]{0:T(128)} %row_ref.3, s32[4]{0:T(128)} %crossover_ref.1, bf16[4,2,16,256]{3,2,1,0:T(8,128)(2,1)} %pairs.1.partial_ref, f32[32,256]{1,0:T(8,128)} %get-tuple-element.12.spectrum_ref, f32[1,16,2,256]{3,2,1,0:T(2,128)} %band_ref.3, bf16[2,2,512,256]{3,2,1,0:T(8,128)(2,1)} %constant.2.clone.table_hbm), custom_call_target="tpu_custom_call" | custom-call | tf_op jit(solution)/shard_map/merge/pallas_call | solution.py:399
  34.4 1.4 %copy.13 = f32[1,16,2,256]{3,2,1,0:T(2,128)} copy(f32[1,16,2,256]{3,2,1,0:T(2,128)} %merge.1) | data formatting | bytes 65536

commit v2 on v1

--- a/solution.py
+++ b/solution.py
@@ -43,11 +43,19 @@
     return dot(head, upper) + (dot(head, lower) + dot(tail, upper))
 
 
-def greet(peers):
+def hail(peers):
     barrier = pltpu.get_barrier_semaphore()
     for peer in peers:
         pl.semaphore_signal(barrier, inc=1, device_id=peer, device_id_type=MESH)
-    pl.semaphore_wait(barrier, len(peers))
+
+
+def await_all(peers):
+    pl.semaphore_wait(pltpu.get_barrier_semaphore(), len(peers))
+
+
+def greet(peers):
+    hail(peers)
+    await_all(peers)
 
 
 def others(me, count):
@@ -56,6 +64,9 @@
 
 def gather_kernel(
     count,
+    row_ref,
+    blocks_ref,
+    covered_ref,
     strain_ref,
     scale_ref,
     mechanism_ref,
@@ -72,10 +83,14 @@
     table_buf,
     band_send,
     band_peer,
+    slip_pack,
+    onset_pack,
     local_sem,
     strain_sem,
     send_sem,
     recv_sem,
+    pass_sem,
+    passed_sem,
 ):
     me = lax.axis_index("pt")
     part = lax.axis_index("cmp")
@@ -92,23 +107,58 @@
         copy = pltpu.make_async_copy(strain_ref.at[rows], strain_buf.at[rows], strain_sem.at[b])
         copy.start()
         strain_copies.append(copy)
-    table_copy = pltpu.make_async_copy(table_hbm.at[part], table_buf, local_sem.at[2])
+    table_copy = pltpu.make_async_copy(table_hbm.at[part], table_buf, local_sem)
     table_copy.start()
-    keep = [
-        pltpu.make_async_copy(slip_ref, slips_ref.at[pl.ds(me, 1)], local_sem.at[0]),
-        pltpu.make_async_copy(onset_ref, onsets_ref.at[pl.ds(me, 1)], local_sem.at[1]),
-    ]
-    for copy in keep:
-        copy.start()
     for c in range(2):
         band_send[pl.ds(c * variations, variations), :] = band_ref[0, :, c, :]
-    greet(others(me, count) + [partner])
+    peers = others(me, count)
+    hail(peers + [partner])
+    rupture = row_ref[me]
+    covered = covered_ref[rupture]
+    spread = variations // 2
+    first_part = part == 0
+
+    slot_total = blocks_ref.shape[1]
+    whole = [
+        (
+            onset_ref[0, :, slot * block : (slot + 1) * block],
+            slip_ref[0, :, slot * block : (slot + 1) * block].astype(jnp.float32),
+        )
+        for slot in range(slot_total)
+    ]
+    halved = [
+        tuple(jnp.where(first_part, tile[:spread], tile[spread:]) for tile in pair)
+        for pair in whole
+    ]
+
+    def packed(target, tiles):
+        lowest = target * blocks_here
+        totals = [[jnp.zeros_like(tile) for tile in tiles[0]] for k in range(blocks_here)]
+        found = jnp.int32(0)
+        for slot in range(slot_total):
+            named = blocks_ref[rupture, slot]
+            live = (slot < covered) & (named >= lowest) & (named < lowest + blocks_here)
+            for k in range(min(blocks_here, slot + 1)):
+                share = (live & (found == k)).astype(jnp.int32).astype(jnp.float32)
+                for which in range(2):
+                    totals[k][which] = totals[k][which] + share * tiles[slot][which]
+            found = found + live.astype(jnp.int32)
+        return totals
+
+    def pack(step, carry):
+        for k, (onset, slip) in enumerate(packed(lax.rem(me + 1 + step, count), halved)):
+            onset_pack[step, k] = onset
+            slip_pack[step, k] = slip.astype(slip_pack.dtype)
+        return carry
+
+    lax.fori_loop(0, count - 1, pack, 0)
+    await_all(peers + [partner])
     sends = []
-    for step, peer in enumerate(others(me, count)):
-        for which, (source, target) in enumerate(((onset_ref, onsets_ref), (slip_ref, slips_ref))):
+    for step, peer in enumerate(peers):
+        for which, (source, target) in enumerate(((onset_pack, onsets_ref), (slip_pack, slips_ref))):
             copy = pltpu.make_async_remote_copy(
-                src_ref=source,
-                dst_ref=target.at[pl.ds(me, 1)],
+                src_ref=source.at[step],
+                dst_ref=target.at[me, part],
                 send_sem=send_sem.at[2 * step + which],
                 recv_sem=recv_sem.at[2 * step + which],
                 device_id=peer,
@@ -125,6 +175,10 @@
         device_id_type=MESH,
     )
     band_copy.start()
+    for k, (onset, slip) in enumerate(packed(me, whole)):
+        for h in range(2):
+            slips_ref[me, h, k] = slip[h * spread : (h + 1) * spread].astype(slips_ref.dtype)
+            onsets_ref[me, h, k] = onset[h * spread : (h + 1) * spread]
 
     low_lanes = lax.broadcasted_iota(jnp.int32, (block, bins), 1) < half
     for b in range(blocks_here):
@@ -158,6 +212,22 @@
                     low_lanes, first, second
                 ).astype(jnp.bfloat16)
 
+    passes = []
+    for step in range(count - 1):
+        source_row = lax.rem(me + count - 1 - step, count)
+        for which, target in enumerate((onsets_ref, slips_ref)):
+            sends[2 * step + which].wait_recv()
+            held = target.at[source_row, part]
+            copy = pltpu.make_async_remote_copy(
+                src_ref=held,
+                dst_ref=held,
+                send_sem=pass_sem.at[2 * step + which],
+                recv_sem=passed_sem.at[2 * step + which],
+                device_id=partner,
+                device_id_type=MESH,
+            )
+            copy.start()
+            passes.append(copy)
     table_copy.wait()
     band_copy.wait()
     mine = pl.ds(pl.multiple_of(part * own, own), own)
@@ -166,9 +236,9 @@
     spectrum_ref[...] = wide_dot(
         band_send[...], table_buf[0, mine, :], table_buf[1, mine, :], down
     ) + wide_dot(band_peer[...], table_buf[0, theirs, :], table_buf[1, theirs, :], down)
-    for copy in keep:
-        copy.wait()
     for copy in sends:
+        copy.wait_send()
+    for copy in passes:
         copy.wait()
 
 
@@ -193,8 +263,8 @@
     me = lax.axis_index("pt")
     part = lax.axis_index("cmp")
     blocks_here, halves, depth, columns = weights_ref.shape
-    rows, variations, unused = slips_ref.shape
-    block = depth // 2
+    rows, shares, unused, spread, block = slips_ref.shape
+    variations = shares * spread
     bins = columns // 2
     half = bins // 2
     fine_total = 16
@@ -205,14 +275,19 @@
         rupture = row_ref[row]
         total_ref[...] = jnp.zeros_like(total_ref)
 
-        def one_slot(slot, carry):
+        def one_slot(slot, found_here):
             local = blocks_ref[rupture, slot] - lowest
-
-            @pl.when((local >= 0) & (local < blocks_here))
+            live = (local >= 0) & (local < blocks_here)
+
+            @pl.when(live)
             def _():
-                lanes = pl.ds(pl.multiple_of(slot * block, block), block)
-                angle = onsets_ref[row, :, lanes] * step_angle
-                amplitude = slips_ref[row, :, lanes].astype(jnp.float32)
+                angle = step_angle * jnp.concatenate(
+                    [onsets_ref[row, h, found_here] for h in range(shares)], axis=0
+                )
+                amplitude = jnp.concatenate(
+                    [slips_ref[row, h, found_here].astype(jnp.float32) for h in range(shares)],
+                    axis=0,
+                )
                 powers = [None, (jnp.cos(angle), jnp.sin(angle))]
                 for k in range(2, fine_total + 1):
                     powers.append(turn(powers[k // 2], powers[k - k // 2]))
@@ -252,9 +327,9 @@
                         coarse = turn(coarse, leap)
                     total_ref[which] += found
 
-            return carry
-
-        lax.fori_loop(0, covered_ref[rupture], one_slot, 0)
+            return found_here + live.astype(jnp.int32)
+
+        lax.fori_loop(0, covered_ref[rupture], one_slot, jnp.int32(0))
         partial_ref[row] = total_ref[...].astype(jnp.bfloat16)
         return carry
 
@@ -364,30 +439,46 @@
     smem = pl.BlockSpec(memory_space=SMEM)
     anywhere = pl.BlockSpec(memory_space=pl.ANY)
     copies = 2 * (count - 1) + 1
+    share = (blocks_here, variations // 2, block)
     weights, slips, onsets, band_spectrum = pl.pallas_call(
         functools.partial(gather_kernel, count),
         out_shape=(
             jax.ShapeDtypeStruct((blocks_here, 2, 2 * block, 2 * bins), jnp.bfloat16),
-            jax.ShapeDtypeStruct((rows, variations, slots), slip_amplitude.dtype),
-            jax.ShapeDtypeStruct((rows, variations, slots), onset_time.dtype),
+            jax.ShapeDtypeStruct((rows, 2) + share, slip_amplitude.dtype),
+            jax.ShapeDtypeStruct((rows, 2) + share, onset_time.dtype),
             jax.ShapeDtypeStruct((2 * variations, 2 * bins), jnp.float32),
         ),
-        in_specs=[anywhere, vmem, vmem, vmem, vmem, vmem, anywhere],
-        out_specs=(vmem, anywhere, anywhere, vmem),
+        in_specs=[smem, smem, smem, anywhere, vmem, vmem, vmem, vmem, vmem, anywhere],
+        out_specs=(vmem, vmem, vmem, vmem),
         scratch_shapes=[
             VMEM(strain_green.shape, strain_green.dtype),
             VMEM((block * 24, bins), jnp.float32),
             VMEM((2, samples, 2 * bins), jnp.bfloat16),
             VMEM((2 * variations, own), jnp.float32),
             VMEM((2 * variations, own), jnp.float32),
-            pltpu.SemaphoreType.DMA((3,)),
+            VMEM((count - 1,) + share, slip_amplitude.dtype),
+            VMEM((count - 1,) + share, onset_time.dtype),
+            pltpu.SemaphoreType.DMA(()),
             pltpu.SemaphoreType.DMA((blocks_here,)),
             pltpu.SemaphoreType.DMA((copies,)),
             pltpu.SemaphoreType.DMA((copies,)),
+            pltpu.SemaphoreType.DMA((copies - 1,)),
+            pltpu.SemaphoreType.DMA((copies - 1,)),
         ],
         compiler_params=pltpu.CompilerParams(collective_id=0, has_side_effects=True),
         name="gather",
-    )(strain_green, green_scale, mechanism, slip_amplitude, onset_time, high_band, tables)
+    )(
+        rupture_row,
+        rupture_blocks,
+        block_count,
+        strain_green,
+        green_scale,
+        mechanism,
+        slip_amplitude,
+        onset_time,
+        high_band,
+        tables,
+    )
     partial_spectra = pl.pallas_call(
         functools.partial(pair_kernel, 2.0 * math.pi / samples),
         out_shape=jax.ShapeDtypeStruct((rows, 2, variations, 2 * bins), jnp.bfloat16),

time: 36 us -> 27.7 us (0.77)
  Pallas kernels: 34.4 us -> 25.9 us
    pallas_call x1, Pallas kernels: 18.4 us -> 12.8 us  [body(): pl.pallas_call(functools.partial(gather_kernel, count), out_shape=(jax.Sh...]
    pallas_call x1, Pallas kernels: 12.4 us -> 9.12 us  [body(): pl.pallas_call(functools.partial(merge_kernel, count), out_shape=jax.Shap...]
    pallas_call x1, Pallas kernels: 3.55 us -> 3.96 us  [body(): pl.pallas_call(functools.partial(pair_kernel, 2.0 * math.pi / samples), o...]
where the time goes in v2:
time: 27.7 us; the launch traced here: 27.3 us
  Pallas kernels  25.9 us (94%)
  local copies, waits for them, and re-layouts  1.38 us (5%)
    pallas_call x1, Pallas kernels, body(): pl.pallas_call(functools.partial(gather_kernel, count), out_shape=(jax.Sh...  12.8 us
    pallas_call x1, Pallas kernels, body(): pl.pallas_call(functools.partial(merge_kernel, count), out_shape=jax.Shap...  9.12 us
    pallas_call x1, Pallas kernels, body(): pl.pallas_call(functools.partial(pair_kernel, 2.0 * math.pi / samples), o...  3.96 us
    unnamed x1, local copies, waits for them, and re-layouts  1.38 us

profile of v2, /device:TPU:0, one launch (start us, length us, event | category | flops | bytes accessed | tf_op | source)
XLA Modules:
  0.0 27.3 jit_solution(14711828746761333526)
XLA Ops:
  0.0 12.8 %gather.1 = (bf16[5,2,256,256]{3,2,1,0:T(8,128)(2,1)}, bf16[4,2,5,8,128]{4,3,2,1,0:T(8,128)(2,1)}, f32[4,2,5,8,128]{4,3,2,1,0:T(8,128)}, f32[32,256]{1,0:T(8,128)}) custom-call(s32[4]{0:T(128)} %row_ref.5, s32[4,12]{1,0:T(4,128)} %blocks_ref.3, s32[4]{0:T(128)} %covered_ref.3, bf16[640,24,128]{2,1,0:T(8,128)(2,1)} %strain_ref.1, f32[5,24]{1,0:T(8,128)} %scale_ref.1, ...), custom_call_target="tpu_custom_call" | custom-call | tf_op jit(solution)/shard_map/gather/pallas_call | solution.py:443
  12.8 4.0 %pairs.1.partial_ref = bf16[4,2,16,256]{3,2,1,0:T(8,128)(2,1)} custom-call(s32[4]{0:T(128)} %row_ref.5, s32[4,12]{1,0:T(4,128)} %blocks_ref.3, s32[4]{0:T(128)} %covered_ref.3, bf16[5,2,256,256]{3,2,1,0:T(8,128)(2,1)} %get-tuple-element.9.weights_ref, bf16[4,2,5,8,128]{4,3,2,1,0:T(8,128)(2,1)} %get-tuple-element.10.slips_ref, ...), custom_call_target="tpu_custom_call" | custom-call | tf_op jit(solution)/shard_map/pairs/pallas_call | solution.py:482
  16.8 9.1 %merge.1 = f32[1,16,2,256]{3,2,1,0:T(2,128)} custom-call(s32[4]{0:T(128)} %row_ref.5, s32[4]{0:T(128)} %crossover_ref.1, bf16[4,2,16,256]{3,2,1,0:T(8,128)(2,1)} %pairs.1.partial_ref, f32[32,256]{1,0:T(8,128)} %get-tuple-element.12.spectrum_ref, f32[1,16,2,256]{3,2,1,0:T(2,128)} %band_ref.3, bf16[2,2,512,256]{3,2,1,0:T(8,128)(2,1)} %constant.2.clone.table_hbm), custom_call_target="tpu_custom_call" | custom-call | tf_op jit(solution)/shard_map/merge/pallas_call | solution.py:490
  25.9 1.4 %copy.13 = f32[1,16,2,256]{3,2,1,0:T(2,128)} copy(f32[1,16,2,256]{3,2,1,0:T(2,128)} %merge.1) | data formatting | bytes 65536

commit v3 on v2

--- a/solution.py
+++ b/solution.py
@@ -78,10 +78,11 @@
     slips_ref,
     onsets_ref,
     spectrum_ref,
+    band_send,
+    final_table,
     strain_buf,
     wide_buf,
     table_buf,
-    band_send,
     band_peer,
     slip_pack,
     onset_pack,
@@ -107,8 +108,18 @@
         copy = pltpu.make_async_copy(strain_ref.at[rows], strain_buf.at[rows], strain_sem.at[b])
         copy.start()
         strain_copies.append(copy)
-    table_copy = pltpu.make_async_copy(table_hbm.at[part], table_buf, local_sem)
+    table_copy = pltpu.make_async_copy(table_hbm.at[part], table_buf, local_sem.at[0])
     table_copy.start()
+    mine = pl.ds(pl.multiple_of(part * own, own), own)
+    theirs = pl.ds(pl.multiple_of((1 - part) * own, own), own)
+    final_copies = []
+    for p in range(final_table.shape[0]):
+        for which in range(2):
+            copy = pltpu.make_async_copy(
+                table_hbm.at[p, which, mine], final_table.at[p, which], local_sem.at[1 + 2 * p + which]
+            )
+            copy.start()
+            final_copies.append(copy)
     for c in range(2):
         band_send[pl.ds(c * variations, variations), :] = band_ref[0, :, c, :]
     peers = others(me, count)
@@ -230,12 +241,12 @@
             passes.append(copy)
     table_copy.wait()
     band_copy.wait()
-    mine = pl.ds(pl.multiple_of(part * own, own), own)
-    theirs = pl.ds(pl.multiple_of((1 - part) * own, own), own)
     down = ((1,), (0,))
     spectrum_ref[...] = wide_dot(
         band_send[...], table_buf[0, mine, :], table_buf[1, mine, :], down
     ) + wide_dot(band_peer[...], table_buf[0, theirs, :], table_buf[1, theirs, :], down)
+    for copy in final_copies:
+        copy.wait()
     for copy in sends:
         copy.wait_send()
     for copy in passes:
@@ -338,30 +349,23 @@
 
 def merge_kernel(
     count,
+    samples,
     row_ref,
     crossover_ref,
     partial_ref,
     spectrum_ref,
-    band_ref,
-    table_hbm,
-    out_ref,
+    excess_ref,
     arrived,
-    table_buf,
-    low_send,
-    low_peer,
-    local_sem,
+    excess_send,
     send_sem,
     recv_sem,
 ):
     me = lax.axis_index("pt")
     part = lax.axis_index("cmp")
     partner = {"cmp": 1 - part}
-    own = band_ref.shape[3]
     bins = partial_ref.shape[3] // 2
     half = bins // 2
     variations = partial_ref.shape[2]
-    table_copy = pltpu.make_async_copy(table_hbm.at[part], table_buf, local_sem)
-    table_copy.start()
     greet(others(me, count) + [partner])
     sends = []
     for step, peer in enumerate(others(me, count)):
@@ -380,37 +384,47 @@
     frequency_id = part * bins + (column // bins) * half + column % half
     frequency = frequency_id.astype(jnp.float32)
     taper = jnp.clip((crossing - frequency) / taper_width + 0.5, 0.0, 1.0)
-    weight = taper * jnp.where(frequency_id == 0, 1.0, 2.0) / table_buf.shape[1]
-    table_copy.wait()
+    weight = taper * jnp.where(frequency_id == 0, 1.0, 2.0) / samples
     total = partial_ref[me].astype(jnp.float32)
     for step, copy in enumerate(sends):
-        copy.wait()
+        copy.wait_recv()
         total = total + arrived[step].astype(jnp.float32)
-    excess = []
     for c in range(2):
         lanes = slice(c * bins, (c + 1) * bins)
+        here = pl.ds(c * variations, variations)
         spectrum = jnp.concatenate([total[0][:, lanes], total[1][:, lanes]], axis=1)
-        here = pl.ds(c * variations, variations)
-        excess.append((spectrum - spectrum_ref[here, :]) * weight)
-    rows = jnp.concatenate(excess, axis=0)
-    mine = pl.ds(pl.multiple_of(part * own, own), own)
-    theirs = pl.ds(pl.multiple_of((1 - part) * own, own), own)
-    across = ((1,), (1,))
-    low_send[...] = wide_dot(rows, table_buf[0, theirs, :], table_buf[1, theirs, :], across)
+        excess_send[here, :] = (spectrum - spectrum_ref[here, :]) * weight
     exchange = pltpu.make_async_remote_copy(
-        src_ref=low_send,
-        dst_ref=low_peer,
+        src_ref=excess_send,
+        dst_ref=excess_ref.at[1],
         send_sem=send_sem.at[count - 1],
         recv_sem=recv_sem.at[count - 1],
         device_id=partner,
         device_id_type=MESH,
     )
     exchange.start()
-    low = wide_dot(rows, table_buf[0, mine, :], table_buf[1, mine, :], across)
+    excess_ref[0] = excess_send[...]
+    for copy in sends:
+        copy.wait_send()
     exchange.wait()
-    low = low + low_peer[...]
+
+
+def final_kernel(excess_ref, band_ref, table_ref, out_ref):
+    part = lax.axis_index("cmp")
+    variations = out_ref.shape[1]
+    across = ((1,), (1,))
+    low = band_ref[...]
+    for which in range(2):
+        source = lax.rem(part + which, 2)
+        low = low + wide_dot(
+            excess_ref[which], table_ref[source, 0], table_ref[source, 1], across
+        )
     for c in range(2):
-        out_ref[0, :, c, :] = band_ref[0, :, c, :] + low[c * variations : (c + 1) * variations]
+        out_ref[0, :, c, :] = low[c * variations : (c + 1) * variations]
+
+
+def stay(array):
+    return pltpu.with_memory_space_constraint(array, VMEM)
 
 
 def body(
@@ -437,28 +451,30 @@
     tables = jnp.asarray(basis_tables(bins, parts, samples))
     vmem = pl.BlockSpec(memory_space=VMEM)
     smem = pl.BlockSpec(memory_space=SMEM)
-    anywhere = pl.BlockSpec(memory_space=pl.ANY)
+    anywhere = pl.BlockSpec(memory_space=pltpu.HBM)
+    grant = 24 * 1024 * 1024
     copies = 2 * (count - 1) + 1
     share = (blocks_here, variations // 2, block)
-    weights, slips, onsets, band_spectrum = pl.pallas_call(
+    weights, slips, onsets, band_spectrum, band_rows, final_table = pl.pallas_call(
         functools.partial(gather_kernel, count),
         out_shape=(
-            jax.ShapeDtypeStruct((blocks_here, 2, 2 * block, 2 * bins), jnp.bfloat16),
-            jax.ShapeDtypeStruct((rows, 2) + share, slip_amplitude.dtype),
-            jax.ShapeDtypeStruct((rows, 2) + share, onset_time.dtype),
-            jax.ShapeDtypeStruct((2 * variations, 2 * bins), jnp.float32),
+            VMEM((blocks_here, 2, 2 * block, 2 * bins), jnp.bfloat16),
+            VMEM((rows, 2) + share, slip_amplitude.dtype),
+            VMEM((rows, 2) + share, onset_time.dtype),
+            VMEM((2 * variations, 2 * bins), jnp.float32),
+            VMEM((2 * variations, own), jnp.float32),
+            VMEM((parts, 2, own, 2 * bins), jnp.bfloat16),
         ),
         in_specs=[smem, smem, smem, anywhere, vmem, vmem, vmem, vmem, vmem, anywhere],
-        out_specs=(vmem, vmem, vmem, vmem),
+        out_specs=(vmem,) * 6,
         scratch_shapes=[
             VMEM(strain_green.shape, strain_green.dtype),
             VMEM((block * 24, bins), jnp.float32),
             VMEM((2, samples, 2 * bins), jnp.bfloat16),
             VMEM((2 * variations, own), jnp.float32),
-            VMEM((2 * variations, own), jnp.float32),
             VMEM((count - 1,) + share, slip_amplitude.dtype),
             VMEM((count - 1,) + share, onset_time.dtype),
-            pltpu.SemaphoreType.DMA(()),
+            pltpu.SemaphoreType.DMA((1 + 2 * parts,)),
             pltpu.SemaphoreType.DMA((blocks_here,)),
             pltpu.SemaphoreType.DMA((copies,)),
             pltpu.SemaphoreType.DMA((copies,)),
@@ -481,29 +497,35 @@
     )
     partial_spectra = pl.pallas_call(
         functools.partial(pair_kernel, 2.0 * math.pi / samples),
-        out_shape=jax.ShapeDtypeStruct((rows, 2, variations, 2 * bins), jnp.bfloat16),
+        out_shape=VMEM((rows, 2, variations, 2 * bins), jnp.bfloat16),
         in_specs=[smem, smem, smem, vmem, vmem, vmem],
         out_specs=vmem,
         scratch_shapes=[VMEM((2, variations, 2 * bins), jnp.float32)],
+        compiler_params=pltpu.CompilerParams(vmem_limit_bytes=grant),
         name="pairs",
-    )(rupture_row, rupture_blocks, block_count, weights, slips, onsets)
-    return pl.pallas_call(
-        functools.partial(merge_kernel, count),
-        out_shape=jax.ShapeDtypeStruct(high_band.shape, high_band.dtype),
-        in_specs=[smem, smem, vmem, vmem, vmem, anywhere],
+    )(rupture_row, rupture_blocks, block_count, stay(weights), stay(slips), stay(onsets))
+    excess = pl.pallas_call(
+        functools.partial(merge_kernel, count, samples),
+        out_shape=VMEM((2, 2 * variations, 2 * bins), jnp.float32),
+        in_specs=[smem, smem, vmem, vmem],
         out_specs=vmem,
         scratch_shapes=[
             VMEM((count - 1, 2, variations, 2 * bins), jnp.bfloat16),
-            VMEM((2, samples, 2 * bins), jnp.bfloat16),
-            VMEM((2 * variations, own), jnp.float32),
-            VMEM((2 * variations, own), jnp.float32),
-            pltpu.SemaphoreType.DMA(()),
+            VMEM((2 * variations, 2 * bins), jnp.float32),
             pltpu.SemaphoreType.DMA((count,)),
             pltpu.SemaphoreType.DMA((count,)),
         ],
-        compiler_params=pltpu.CompilerParams(collective_id=1, has_side_effects=True),
+        compiler_params=pltpu.CompilerParams(collective_id=1, has_side_effects=True, vmem_limit_bytes=grant),
         name="merge",
-    )(rupture_row, crossover, partial_spectra, band_spectrum, high_band, tables)
+    )(rupture_row, crossover, stay(partial_spectra), stay(band_spectrum))
+    return pl.pallas_call(
+        final_kernel,
+        out_shape=jax.ShapeDtypeStruct(high_band.shape, high_band.dtype),
+        in_specs=[vmem, vmem, vmem],
+        out_specs=vmem,
+        compiler_params=pltpu.CompilerParams(vmem_limit_bytes=grant),
+        name="final",
+    )(stay(excess), stay(band_rows), stay(final_table))
 
 
 def solution(mesh):

time: 27.7 us -> 23.4 us (0.84)
  Pallas kernels: 25.9 us -> 23 us
  local copies, waits for them, and re-layouts: 1.38 us -> 0.01 us
    pallas_call x1, Pallas kernels: 3.96 us -> 2.54 us  [body(): pl.pallas_call(functools.partial(pair_kernel, 2.0 * math.pi / samples), o...]
    pallas_call x2 -> x3, Pallas kernels: 21.9 us -> 20.5 us  [the longest x1 11.7 us: body(): pl.pallas_call(functools.partial(gather_kernel, count), out_shape=(VMEM((...]
    unnamed x1 -> x8, local copies, waits for them, and re-layouts: 1.38 us -> 0.01 us
where the time goes in v3:
time: 23.4 us; the launch traced here: 23.1 us
  Pallas kernels  23 us (98%)
    pallas_call x1, Pallas kernels, body(): pl.pallas_call(functools.partial(gather_kernel, count), out_shape=(VMEM((...  11.7 us
    pallas_call x1, Pallas kernels, body(): pl.pallas_call(functools.partial(merge_kernel, count, samples), out_shape...  7.84 us
    pallas_call x1, Pallas kernels, body(): pl.pallas_call(functools.partial(pair_kernel, 2.0 * math.pi / samples), o...  2.54 us
    pallas_call x1, Pallas kernels, body(): pl.pallas_call(final_kernel, out_shape=jax.ShapeDtypeStruct(high_band.sha...  0.97 us

profile of v3, /device:TPU:0, one launch (start us, length us, event | category | flops | bytes accessed | tf_op | source)
XLA Modules:
  0.0 23.1 jit_solution(10002095818628089668)
XLA Ops:
  0.0 0.0 copy-start.1
  0.0 0.0 copy-start.2
  0.0 0.0 copy-start
  0.0 0.0 copy-start.3
  0.0 11.7 %gather.1 = (bf16[5,2,256,256]{3,2,1,0:T(8,128)(2,1)S(1)}, bf16[4,2,5,8,128]{4,3,2,1,0:T(8,128)(2,1)S(1)}, f32[4,2,5,8,128]{4,3,2,1,0:T(8,128)S(1)}, f32[32,256]...) custom-call(s32[4]{0:T(128)} %row_ref.5, s32[4,12]{1,0:T(4,128)} %blocks_ref.3, ...), custom_call_target="tpu_custom_call" | custom-call | tf_op jit(solution)/shard_map/gather/pallas_call | solution.py:458
  11.7 0.0 copy-done.1
  11.7 0.0 copy-done.2
  11.7 0.0 copy-done
  11.7 2.5 %pairs.1.partial_ref = bf16[4,2,16,256]{3,2,1,0:T(8,128)(2,1)S(1)} custom-call(s32[4]{0:T(128)S(1)} %copy-done.1, s32[4,12]{1,0:T(4,128)S(1)} %copy-done, s32[4]{0:T(128)S(1)} %copy-done.2, bf16[5,2,256,256]{3,2,1,0:T(8,128)(2,1)S(1)} %get-tuple-element.11.weights_ref, bf16[4,2,5,8,128]{4,3,2,1,0:T(8,128)(2,1)S(1)} %get-tuple-element.12.slips_ref, ...), custom_call_target="tpu_custom_call" | custom-call | tf_op jit(solution)/shard_map/pairs/pallas_call | solution.py:498
  14.3 0.0 copy-done.3
  14.3 7.8 %merge.1.excess_ref = f32[2,32,256]{2,1,0:T(8,128)S(1)} custom-call(s32[4]{0:T(128)S(1)} %copy-done.1, s32[4]{0:T(128)S(1)} %copy-done.3, bf16[4,2,16,256]{3,2,1,0:T(8,128)(2,1)S(1)} %pairs.1.partial_ref, f32[32,256]{1,0:T(8,128)S(1)} %get-tuple-element.14.spectrum_ref), custom_call_target="tpu_custom_call" | custom-call | tf_op jit(solution)/shard_map/merge/pallas_call | solution.py:507
  22.1 1.0 %final.1 = f32[1,16,2,256]{3,2,1,0:T(2,128)} custom-call(f32[2,32,256]{2,1,0:T(8,128)S(1)} %merge.1.excess_ref, f32[32,256]{1,0:T(8,128)S(1)} %get-tuple-element.15.band_ref, bf16[2,2,256,256]{3,2,1,0:T(8,128)(2,1)S(1)} %get-tuple-element.16.table_ref), custom_call_target="tpu_custom_call" | custom-call | tf_op jit(solution)/shard_map/final/pallas_call | solution.py:521
Async XLA Ops:
  0.0 11.7 %copy-start.1 = (s32[4]{0:T(128)S(1)}, s32[4]{0:T(128)}, u32[]{:S(2)}) copy-start(s32[4]{0:T(128)} %row_ref.5) | copy-start | bytes 52
  0.0 11.7 %copy-start.2 = (s32[4]{0:T(128)S(1)}, s32[4]{0:T(128)}, u32[]{:S(2)}) copy-start(s32[4]{0:T(128)} %covered_ref.3) | copy-start | bytes 52
  0.0 11.7 %copy-start = (s32[4,12]{1,0:T(4,128)S(1)}, s32[4,12]{1,0:T(4,128)}, u32[]{:S(2)}) copy-start(s32[4,12]{1,0:T(4,128)} %blocks_ref.3) | copy-start | bytes 580
  0.0 14.3 %copy-start.3 = (s32[4]{0:T(128)S(1)}, s32[4]{0:T(128)}, u32[]{:S(2)}) copy-start(s32[4]{0:T(128)} %crossover_ref.1) | copy-start | bytes 52

commit v4 on v3

--- a/solution.py
+++ b/solution.py
@@ -67,12 +67,13 @@
     row_ref,
     blocks_ref,
     covered_ref,
+    crossover_ref,
     strain_ref,
-    scale_ref,
-    mechanism_ref,
-    slip_ref,
-    onset_ref,
-    band_ref,
+    scale_hbm,
+    mechanism_hbm,
+    slip_hbm,
+    onset_hbm,
+    band_hbm,
     table_hbm,
     weights_ref,
     slips_ref,
@@ -80,6 +81,12 @@
     spectrum_ref,
     band_send,
     final_table,
+    weight_ref,
+    scale_ref,
+    mechanism_ref,
+    slip_ref,
+    onset_ref,
+    band_ref,
     strain_buf,
     wide_buf,
     table_buf,
@@ -87,6 +94,7 @@
     slip_pack,
     onset_pack,
     local_sem,
+    load_sem,
     strain_sem,
     send_sem,
     recv_sem,
@@ -102,6 +110,22 @@
     half = bins // 2
     own = band_ref.shape[3]
     variations = band_ref.shape[1]
+    samples = own * final_table.shape[0]
+    peers = others(me, count)
+    hail(peers + [partner])
+    loads = []
+    for k, (source, target) in enumerate(
+        (
+            (slip_hbm, slip_ref),
+            (onset_hbm, onset_ref),
+            (band_hbm, band_ref),
+            (mechanism_hbm, mechanism_ref),
+            (scale_hbm, scale_ref),
+        )
+    ):
+        copy = pltpu.make_async_copy(source, target, load_sem.at[k])
+        copy.start()
+        loads.append(copy)
     strain_copies = []
     for b in range(blocks_here):
         rows = pl.ds(b * block, block)
@@ -120,10 +144,8 @@
             )
             copy.start()
             final_copies.append(copy)
-    for c in range(2):
-        band_send[pl.ds(c * variations, variations), :] = band_ref[0, :, c, :]
-    peers = others(me, count)
-    hail(peers + [partner])
+    loads[0].wait()
+    loads[1].wait()
     rupture = row_ref[me]
     covered = covered_ref[rupture]
     spread = variations // 2
@@ -177,6 +199,9 @@
             )
             copy.start()
             sends.append(copy)
+    loads[2].wait()
+    for c in range(2):
+        band_send[pl.ds(c * variations, variations), :] = band_ref[0, :, c, :]
     band_copy = pltpu.make_async_remote_copy(
         src_ref=band_send,
         dst_ref=band_peer,
@@ -191,6 +216,14 @@
             slips_ref[me, h, k] = slip[h * spread : (h + 1) * spread].astype(slips_ref.dtype)
             onsets_ref[me, h, k] = onset[h * spread : (h + 1) * spread]
 
+    crossing = crossover_ref[rupture].astype(jnp.float32)
+    column = lax.broadcasted_iota(jnp.int32, weight_ref.shape, 1)
+    frequency_id = part * bins + (column // bins) * half + column % half
+    frequency = frequency_id.astype(jnp.float32)
+    taper = jnp.clip((crossing - frequency) / taper_width + 0.5, 0.0, 1.0)
+    weight_ref[...] = taper * jnp.where(frequency_id == 0, 1.0, 2.0) / samples
+    loads[3].wait()
+    loads[4].wait()
     low_lanes = lax.broadcasted_iota(jnp.int32, (block, bins), 1) < half
     for b in range(blocks_here):
         strain_copies[b].wait()
@@ -349,10 +382,8 @@
 
 def merge_kernel(
     count,
-    samples,
-    row_ref,
-    crossover_ref,
     partial_ref,
+    weight_ref,
     spectrum_ref,
     excess_ref,
     arrived,
@@ -364,7 +395,6 @@
     part = lax.axis_index("cmp")
     partner = {"cmp": 1 - part}
     bins = partial_ref.shape[3] // 2
-    half = bins // 2
     variations = partial_ref.shape[2]
     greet(others(me, count) + [partner])
     sends = []
@@ -379,12 +409,7 @@
         )
         copy.start()
         sends.append(copy)
-    crossing = crossover_ref[row_ref[me]].astype(jnp.float32)
-    column = lax.broadcasted_iota(jnp.int32, (variations, 2 * bins), 1)
-    frequency_id = part * bins + (column // bins) * half + column % half
-    frequency = frequency_id.astype(jnp.float32)
-    taper = jnp.clip((crossing - frequency) / taper_width + 0.5, 0.0, 1.0)
-    weight = taper * jnp.where(frequency_id == 0, 1.0, 2.0) / samples
+    weight = weight_ref[...]
     total = partial_ref[me].astype(jnp.float32)
     for step, copy in enumerate(sends):
         copy.wait_recv()
@@ -455,7 +480,7 @@
     grant = 24 * 1024 * 1024
     copies = 2 * (count - 1) + 1
     share = (blocks_here, variations // 2, block)
-    weights, slips, onsets, band_spectrum, band_rows, final_table = pl.pallas_call(
+    weights, slips, onsets, band_spectrum, band_rows, final_table, weight = pl.pallas_call(
         functools.partial(gather_kernel, count),
         out_shape=(
             VMEM((blocks_here, 2, 2 * block, 2 * bins), jnp.bfloat16),
@@ -464,10 +489,16 @@
             VMEM((2 * variations, 2 * bins), jnp.float32),
             VMEM((2 * variations, own), jnp.float32),
             VMEM((parts, 2, own, 2 * bins), jnp.bfloat16),
+            VMEM((variations, 2 * bins), jnp.float32),
         ),
-        in_specs=[smem, smem, smem, anywhere, vmem, vmem, vmem, vmem, vmem, anywhere],
-        out_specs=(vmem,) * 6,
+        in_specs=[smem] * 4 + [anywhere] * 7,
+        out_specs=(vmem,) * 7,
         scratch_shapes=[
+            VMEM(green_scale.shape, green_scale.dtype),
+            VMEM(mechanism.shape, mechanism.dtype),
+            VMEM(slip_amplitude.shape, slip_amplitude.dtype),
+            VMEM(onset_time.shape, onset_time.dtype),
+            VMEM(high_band.shape, high_band.dtype),
             VMEM(strain_green.shape, strain_green.dtype),
             VMEM((block * 24, bins), jnp.float32),
             VMEM((2, samples, 2 * bins), jnp.bfloat16),
@@ -475,6 +506,7 @@
             VMEM((count - 1,) + share, slip_amplitude.dtype),
             VMEM((count - 1,) + share, onset_time.dtype),
             pltpu.SemaphoreType.DMA((1 + 2 * parts,)),
+            pltpu.SemaphoreType.DMA((5,)),
             pltpu.SemaphoreType.DMA((blocks_here,)),
             pltpu.SemaphoreType.DMA((copies,)),
             pltpu.SemaphoreType.DMA((copies,)),
@@ -487,6 +519,7 @@
         rupture_row,
         rupture_blocks,
         block_count,
+        crossover,
         strain_green,
         green_scale,
         mechanism,
@@ -505,9 +538,9 @@
         name="pairs",
     )(rupture_row, rupture_blocks, block_count, stay(weights), stay(slips), stay(onsets))
     excess = pl.pallas_call(
-        functools.partial(merge_kernel, count, samples),
+        functools.partial(merge_kernel, count),
         out_shape=VMEM((2, 2 * variations, 2 * bins), jnp.float32),
-        in_specs=[smem, smem, vmem, vmem],
+        in_specs=[vmem, vmem, vmem],
         out_specs=vmem,
         scratch_shapes=[
             VMEM((count - 1, 2, variations, 2 * bins), jnp.bfloat16),
@@ -517,7 +550,7 @@
         ],
         compiler_params=pltpu.CompilerParams(collective_id=1, has_side_effects=True, vmem_limit_bytes=grant),
         name="merge",
-    )(rupture_row, crossover, stay(partial_spectra), stay(band_spectrum))
+    )(stay(partial_spectra), stay(weight), stay(band_spectrum))
     return pl.pallas_call(
         final_kernel,
         out_shape=jax.ShapeDtypeStruct(high_band.shape, high_band.dtype),

time: 23.4 us -> 22.9 us (0.979); the launches traced: 23.1 us -> 22.9 us
    pallas_call x1, Pallas kernels: 7.84 us -> 6.54 us  [body(): pl.pallas_call(functools.partial(merge_kernel, count), out_shape=VMEM((2,...]
    pallas_call x1, Pallas kernels: 2.54 us -> 3.64 us  [body(): pl.pallas_call(functools.partial(pair_kernel, 2.0 * math.pi / samples), o...]
where the time goes in v4:
time: 22.9 us
  Pallas kernels  22.8 us (100%)
    pallas_call x1, Pallas kernels, body(): pl.pallas_call(functools.partial(gather_kernel, count), out_shape=(VMEM((...  11.7 us
    pallas_call x1, Pallas kernels, body(): pl.pallas_call(functools.partial(merge_kernel, count), out_shape=VMEM((2,...  6.54 us
    pallas_call x1, Pallas kernels, body(): pl.pallas_call(functools.partial(pair_kernel, 2.0 * math.pi / samples), o...  3.64 us
    pallas_call x1, Pallas kernels, body(): pl.pallas_call(final_kernel, out_shape=jax.ShapeDtypeStruct(high_band.sha...  0.98 us

profile of v4, /device:TPU:0, one launch (start us, length us, event | category | flops | bytes accessed | tf_op | source)
XLA Modules:
  0.0 22.9 jit_solution(2979397863373545702)
XLA Ops:
  0.0 0.0 copy-start.2
  0.0 0.0 copy-start
  0.0 0.0 copy-start.1
  0.0 11.7 %gather.1 = (bf16[5,2,256,256]{3,2,1,0:T(8,128)(2,1)S(1)}, bf16[4,2,5,8,128]{4,3,2,1,0:T(8,128)(2,1)S(1)}, f32[4,2,5,8,128]{4,3,2,1,0:T(8,128)S(1)}, f32[32,256]...) custom-call(s32[4]{0:T(128)} %row_ref.3, ...), custom_call_target="tpu_custom_call" | custom-call | tf_op jit(solution)/shard_map/gather/pallas_call | solution.py:483
  11.7 0.0 copy-done.2
  11.7 0.0 copy-done
  11.7 0.0 copy-done.1
  11.7 3.6 %pairs.1.partial_ref = bf16[4,2,16,256]{3,2,1,0:T(8,128)(2,1)S(1)} custom-call(s32[4]{0:T(128)S(1)} %copy-done.1, s32[4,12]{1,0:T(4,128)S(1)} %copy-done, s32[4]{0:T(128)S(1)} %copy-done.2, bf16[5,2,256,256]{3,2,1,0:T(8,128)(2,1)S(1)} %get-tuple-element.12.weights_ref, bf16[4,2,5,8,128]{4,3,2,1,0:T(8,128)(2,1)S(1)} %get-tuple-element.13.slips_ref, ...), custom_call_target="tpu_custom_call" | custom-call | tf_op jit(solution)/shard_map/pairs/pallas_call | solution.py:531
  15.4 6.5 %merge.1.excess_ref = f32[2,32,256]{2,1,0:T(8,128)S(1)} custom-call(bf16[4,2,16,256]{3,2,1,0:T(8,128)(2,1)S(1)} %pairs.1.partial_ref, f32[16,256]{1,0:T(8,128)S(1)} %get-tuple-element.15.weight_ref, f32[32,256]{1,0:T(8,128)S(1)} %get-tuple-element.16.spectrum_ref), custom_call_target="tpu_custom_call" | custom-call | tf_op jit(solution)/shard_map/merge/pallas_call | solution.py:540
  21.9 1.0 %final.1 = f32[1,16,2,256]{3,2,1,0:T(2,128)} custom-call(f32[2,32,256]{2,1,0:T(8,128)S(1)} %merge.1.excess_ref, f32[32,256]{1,0:T(8,128)S(1)} %get-tuple-element.17.band_ref, bf16[2,2,256,256]{3,2,1,0:T(8,128)(2,1)S(1)} %get-tuple-element.18.table_ref), custom_call_target="tpu_custom_call" | custom-call | tf_op jit(solution)/shard_map/final/pallas_call | solution.py:554
Async XLA Ops:
  0.0 11.7 %copy-start.2 = (s32[4]{0:T(128)S(1)}, s32[4]{0:T(128)}, u32[]{:S(2)}) copy-start(s32[4]{0:T(128)} %covered_ref.3) | copy-start | bytes 52
  0.0 11.7 %copy-start = (s32[4,12]{1,0:T(4,128)S(1)}, s32[4,12]{1,0:T(4,128)}, u32[]{:S(2)}) copy-start(s32[4,12]{1,0:T(4,128)} %blocks_ref.3) | copy-start | bytes 580
  0.0 11.7 %copy-start.1 = (s32[4]{0:T(128)S(1)}, s32[4]{0:T(128)}, u32[]{:S(2)}) copy-start(s32[4]{0:T(128)} %row_ref.3) | copy-start | bytes 52
